TPU v7x, 256 devices: a whole 4x4x8 slice. The times are simulated.
256 devices in a mesh: dp: 32 (over z, x_hi, core), space: 8 (over x_lo, y).
Axes of the slice: x: 4 (x_hi: 2, x_lo: 2; x = x_hi * 2 + x_lo), y: 4, z: 8, core: 2. Of those that a mesh axis runs over, the one named last changes fastest.
Arguments:
- volume: bfloat16 [256, 4, 32, 16, 128], P('dp', None, 'space'), may hold values from -8 to 8
- conv_kernel: bfloat16 [32, 108], replicated, may hold values from -0.625 to 0.625
- dense_weight: bfloat16 [512, 128], replicated, may hold values from -0.25 to 0.25
- cotangent: bfloat16 [256, 128], P(('dp', 'space')), may hold values from -6 to 6
Outputs:
- step_conv: float32 [32, 108], replicated
- step_dense: float32 [512, 128], P('space', 'dp')
All inputs are finite; a program needn't handle non-finite values. Where the computation divides by a largest or mean magnitude, that divisor is 1e-20 or more.
Results may differ from a plain program's by a relative error of at most 0.0099.
Values may be sent and summed in bfloat16 or wider, within the bound.
No kernel may reach another device: no remote copies, remote signals or barrier semaphores. Data moves between devices by JAX's collectives and lax.ppermute only.
A program may use at most 64 MiB of HBM per device.

v0:
```python
import jax
import jax.numpy as jnp
from jax import lax
from jax.sharding import PartitionSpec as P

PC = 2
NS_STEPS = 8
LEAK_SLOPE = 0.3
DAMPING = 0.1
KL_BOUND = 0.0001
LEARN_RATE = 0.01
HIGHEST = lax.Precision.HIGHEST
CONTRACT = (((1,), (1,)), ((), ()))
LEADING = (((0,), (0,)), ((), ()))


def spread_2(value, axis, source):
    kept = jnp.where(lax.axis_index(axis) == source, value, 0).astype(value.dtype)
    return lax.psum(kept, axis)


def extended(x, sides, width):
    for axis, dim in sides:
        peers, length = (lax.axis_size(axis), x.shape[dim])
        up = [(i, (i + 1) % peers) for i in range(peers - 1)]
        down = [(j, i) for i, j in up]
        last = lax.slice_in_dim(x, length - width, length, axis=dim)
        initial = lax.slice_in_dim(x, 0, width, axis=dim)
        before = lax.ppermute(last, axis, up)
        after = lax.ppermute(initial, axis, down)
        x = jnp.concatenate([before, x, after], axis=dim)
    return x


def patch_matrix(slab_rim):
    channels, planes_rim, height, length = slab_rim.shape
    planes = planes_rim - 2
    padded = jnp.pad(slab_rim, ((0, 0), (0, 0), (1, 1), (1, 1)))
    pieces = []
    for shift_x in range(3):
        for shift_y in range(3):
            for shift_z in range(3):
                pieces.append(
                    padded[
                        :,
                        shift_x : shift_x + planes,
                        shift_y : shift_y + height,
                        shift_z : shift_z + length,
                    ]
                )
    return jnp.stack(pieces, axis=1).reshape(channels * 27, planes * height * length)


def damped_inverse(factor):
    factor_order = factor.shape[0]
    identity = jnp.eye(factor_order, dtype=jnp.float32)
    damped = factor + DAMPING * jnp.trace(factor) / factor_order * identity
    row_bound = jnp.max(jnp.sum(jnp.abs(damped), axis=1))
    iterate = identity / row_bound
    for newton_step in range(NS_STEPS):
        product = jnp.dot(damped, iterate, precision=HIGHEST)
        iterate = jnp.dot(iterate, 2.0 * identity - product, precision=HIGHEST)
    return iterate


def owned_inverse(factor, owner_index):
    mine = lax.axis_index("dp") == owner_index
    local_inverse = lax.cond(mine, damped_inverse, jnp.zeros_like, factor)
    return spread_2(local_inverse, "dp", owner_index)


def pool_regions(active, planes, height, length):
    shaped = active.reshape(active.shape[0], planes, PC, height // PC, length)
    return jnp.mean(shaped, axis=(1, 3, 4)).reshape(-1)


def dense_moments_of(features, cotangent):
    dense_in = lax.dot_general(features, features, LEADING, preferred_element_type=jnp.float32)
    dense_out = lax.dot_general(cotangent, cotangent, LEADING, preferred_element_type=jnp.float32)
    dense_grad = lax.dot_general(features, cotangent, LEADING, preferred_element_type=jnp.float32)
    return (dense_in, dense_out, dense_grad)


def on_device(volume, conv_kernel, dense_weight, cotangent):
    spaces = lax.axis_size("space")
    groups = lax.axis_size("dp")
    samples, channels, planes, height, length = volume.shape
    filters = conv_kernel.shape[0]
    patch_rows = conv_kernel.shape[1]
    padded = extended(volume, (("space", 2),), 1)

    def forward_pass(moment_in, slab_rim):
        patches = patch_matrix(slab_rim)
        before = jnp.dot(conv_kernel, patches, preferred_element_type=jnp.float32)
        active = jnp.where(before > 0, before, LEAK_SLOPE * before)
        pooled = pool_regions(active, planes, height, length).astype(jnp.bfloat16)
        gram = lax.dot_general(patches, patches, CONTRACT, preferred_element_type=jnp.float32)
        return (moment_in + gram, pooled)

    moment_in, pooled_all = lax.scan(
        forward_pass, jnp.zeros((patch_rows, patch_rows), jnp.float32), padded
    )
    features = lax.all_to_all(pooled_all, "space", split_axis=0, concat_axis=1, tiled=True)
    feature_grad = lax.dot_general(
        cotangent, dense_weight, CONTRACT, preferred_element_type=jnp.float32
    ).astype(jnp.bfloat16)
    returned = lax.all_to_all(feature_grad, "space", split_axis=1, concat_axis=0, tiled=True)

    def backward_pass(totals, pair):
        slab_rim, region_grad = pair
        patches = patch_matrix(slab_rim)
        before = jnp.dot(conv_kernel, patches, preferred_element_type=jnp.float32)
        region_grid = region_grad.astype(jnp.float32).reshape(filters, 1, PC, 1, 1)
        spread = jnp.broadcast_to(region_grid, (filters, planes, PC, height // PC, length)).reshape(
            filters, -1
        )
        signal = (jnp.where(before > 0, 1.0, LEAK_SLOPE) * spread).astype(jnp.bfloat16)
        moment_out = totals[0] + lax.dot_general(
            signal, signal, CONTRACT, preferred_element_type=jnp.float32
        )
        gradient = totals[1] + lax.dot_general(
            signal, patches, CONTRACT, preferred_element_type=jnp.float32
        )
        return ((moment_out, gradient), None)

    start_totals = (
        jnp.zeros((filters, filters), jnp.float32),
        jnp.zeros((filters, patch_rows), jnp.float32),
    )
    (moment_out, conv_sum), unused = lax.scan(backward_pass, start_totals, (padded, returned))
    conv_in, conv_out, conv_grad = lax.psum((moment_in, moment_out, conv_sum), ("dp", "space"))
    total_samples = samples * groups
    cell_count = total_samples * planes * spaces * height * length
    conv_in = conv_in / cell_count
    conv_out = conv_out / cell_count
    conv_grad = conv_grad / cell_count
    all_features, all_cotangent = (
        lax.all_gather(features, ("dp", "space"), axis=0, tiled=True),
        lax.all_gather(cotangent, ("dp", "space"), axis=0, tiled=True),
    )
    dense_in, dense_out, dense_grad = dense_moments_of(all_features, all_cotangent)
    dense_in = dense_in / total_samples
    dense_out = dense_out / total_samples
    dense_grad = dense_grad / total_samples
    factors = (conv_in, conv_out, dense_in, dense_out)
    stride = groups // len(factors)
    inverses = []
    for place in range(4):
        inverses.append(owned_inverse(factors[place], place * stride))
    inv_conv_in, inv_conv_out, inv_dense_in, inv_dense_out = inverses
    delta_conv = jnp.dot(
        jnp.dot(inv_conv_out, conv_grad, precision=HIGHEST), inv_conv_in, precision=HIGHEST
    )
    conv_total = jnp.sum(delta_conv * conv_grad)
    delta_whole = jnp.dot(
        jnp.dot(inv_dense_in, dense_grad, precision=HIGHEST), inv_dense_out, precision=HIGHEST
    )
    dense_total = jnp.sum(delta_whole * dense_grad)
    share_rows = dense_grad.shape[0] // spaces
    share_cols = dense_grad.shape[1] // groups
    first_row = lax.axis_index("space") * share_rows
    first_col = lax.axis_index("dp") * share_cols
    delta_rows = lax.dynamic_slice_in_dim(delta_whole, first_row, share_rows, 0)
    delta_block = lax.dynamic_slice_in_dim(delta_rows, first_col, share_cols, 1)
    scaling = jnp.minimum(
        1.0, jnp.sqrt(KL_BOUND / (LEARN_RATE * LEARN_RATE * (conv_total + dense_total)))
    )
    return (scaling * delta_conv, scaling * delta_block)


def solution(mesh):
    placed = (P("dp", None, "space", None, None), P(), P(), P(("dp", "space"), None))
    return jax.shard_map(
        on_device, mesh=mesh, in_specs=placed, out_specs=(P(), P("space", "dp")), check_vma=False
    )
```

profile of v0, /device:TPU:2, one launch (start us, length us, event | category | flops | bytes accessed | tf_op | source)
XLA Modules:
  0.0 2039.7 jit_solution(5955070597931003601)
XLA Ops:
  8.2 3.5 collective-permute-start
  11.7 4.5 collective-permute-start.1
  17.7 3.8 all-to-all-start
  21.5 619.8 %all-gather.1 = bf16[256,1,128]{2,1,0:T(2,128)(2,1)S(1)} all-gather(bf16[1,1,128]{2,1,0:T(2,128)(2,1)} %bitcast.621), channel_id=1, replica_groups=mesh['dp'=32,'space'=8] {'dp','space'}, dimensions={0}, use_global_device_ids=true | all-gather | bytes 65792 | tf_op jit(solution)/shard_map/all_gather | solution.py:139
  642.7 190.2 %while.30 = (s32[]{:T(128)}, f32[32,32]{1,0:T(8,128)S(1)}, f32[32,108]{1,0:T(8,128)S(1)}, bf16[8,4,6,16,128]{4,3,2,1,0:T(8,128)(2,1)S(1)}, bf16[32,108]{1,0:T(8,...) while((s32[]{:T(128)}, f32[32,32]{1,0:T(8,128)S(1)}, ...), condition=%wide.region_1.2_spmd.clone, body=%wide.region_0.1_spmd.clone.sunk | while | flops 131081024 | bytes 15313904 | solution.py:130
  661.6 2.7 reshape.103
  685.3 2.7 reshape.103
  709.1 2.7 reshape.103
  732.9 2.7 reshape.103
  756.7 2.7 reshape.103
  780.5 2.7 reshape.103
  804.2 2.7 reshape.103
  828.0 2.7 reshape.103
  832.9 185.2 %while.31 = (s32[]{:T(128)}, f32[108,108]{1,0:T(8,128)S(1)}, bf16[8,64]{1,0:T(8,128)(2,1)S(1)}, bf16[8,4,6,16,128]{4,3,2,1,0:T(8,128)(2,1)S(1)}, bf16[32,108]{1,...) while((s32[]{:T(128)}, f32[108,108]{1,0:T(8,128)S(1)}, bf16[8,64]{1,0:T(8,128)(2,1)S(1)}, ...), condition=%wide.region_12.13_spmd.clone, body=%wide.region_10.12_spmd.clone.sunk | while | flops 248798048 | bytes 15895667 | solution.py:100
  851.8 2.7 reshape.105
  944.4 2.7 reshape.105
  967.6 2.7 reshape.105
  990.7 2.7 reshape.105
  1018.7 12.3 all-to-all-start.1
  1031.0 73.1 %all-reduce.2 = (f32[32,32]{1,0:T(8,128)S(1)}, f32[32,108]{1,0:T(8,128)S(1)}, f32[108,108]{1,0:T(8,128)S(1)}) all-reduce(f32[32,32]{1,0:T(8,128)S(1)} %get-tuple-element.174, f32[32,108]{1,0:T(8,128)S(1)} %get-tuple-element.175, f32[108,108]{1,0:T(8,128)S(1)} %get-tuple-element.176), channel_id=1, replica_groups=mesh['dp'=32,'space'=8] {'dp','space'}, use_global_device_ids=true, to_apply=%region_2.3 | all-reduce | flops 16144 | bytes 129152 | tf_op jit(solution)/shard_map/psum | solution.py:131
  1104.2 6.2 conditional.5
  1110.4 614.5 %all-gather = bf16[256,1,512]{2,1,0:T(2,128)(2,1)S(1)} all-gather(bf16[1,1,512]{2,1,0:T(2,128)(2,1)S(1)} %reshape.80), channel_id=1, replica_groups=mesh['dp'=32,'space'=8] {'dp','space'}, dimensions={0}, use_global_device_ids=true | all-gather | bytes 263168 | tf_op jit(solution)/shard_map/all_gather | solution.py:138
  1726.8 129.0 %all-reduce.3 = (f32[32,32]{1,0:T(8,128)S(1)}, f32[108,108]{1,0:T(8,128)S(1)}) all-reduce(f32[32,32]{1,0:T(8,128)S(1)} %broadcast_select_fusion.3, f32[108,108]{1,0:T(8,128)S(1)} %broadcast_select_fusion.2), channel_id=1, replica_groups=mesh['dp'=32,'space'=8] {'dp'}, use_global_device_ids=true, to_apply=%region_8.9 | all-reduce | flops 12688 | bytes 101504 | tf_op jit(solution)/shard_map/psum | solution.py:19
  1857.0 168.8 %all-reduce.7.cloned.1.call-done = (f32[512,512]{1,0:T(8,128)}, f32[128,128]{1,0:T(8,128)}) async-done(((f32[512,512]{1,0:T(8,128)}, f32[128,128]{1,0:T(8,128)}), (f32[512,512]{1,0:T(8,128)}, f32[128,128]{1,0:T(8,128)})) %all-reduce.7.cloned.1.call-update) | async-done | bytes 1114128 | tf_op jit(solution)/shard_map/psum | solution.py:19
  (623 shorter events, 359.5 us)
Async XLA Ops:
  7.2 9.0 copy-start
  8.2 634.0 %collective-permute-start = (bf16[8,4,1,16,128]{4,3,2,1,0:T(8,128)(2,1)S(1)}, bf16[8,4,1,16,128]{4,3,2,1,0:T(8,128)(2,1)S(1)}, u32[]{:S(2)}, u32[]{:S(2)}) collective-permute-start(bf16[8,4,1,16,128]{4,3,2,1,0:T(8,128)(2,1)S(1)} %get-tuple-element.247), channel_id=1, source_target_pairs={{0,1},{1,2},{2,3},{3,4},{4,5},{5,6},{6,7},{8,9},{9,10},{10,11},{11... | collective-permute-start | bytes 393224 | tf_op jit(solution)/shard_map/ppermute | solution.py:29
  11.7 631.0 %collective-permute-start.1 = (bf16[8,4,1,16,128]{4,3,2,1,0:T(8,128)(2,1)S(1)}, bf16[8,4,1,16,128]{4,3,2,1,0:T(8,128)(2,1)S(1)}, u32[]{:S(2)}, u32[]{:S(2)}) collective-permute-start(bf16[8,4,1,16,128]{4,3,2,1,0:T(8,128)(2,1)S(1)} %get-tuple-element.246), channel_id=1, source_target_pairs={{1,0},{2,1},{3,2},{4,3},{5,4},{6,5},{7,6},{9,8},{10,9},{11,10},{12... | collective-permute-start | bytes 393224 | tf_op jit(solution)/shard_map/ppermute | solution.py:30
  17.7 624.5 %all-to-all-start = ((bf16[1,8,64]{2,0,1:T(2,128)(2,1)}), bf16[1,8,64]{2,0,1:T(2,128)(2,1)S(1)}, u32[]{:S(2)}, u32[]{:S(2)}) async-start(bf16[1,8,64]{2,0,1:T(2,128)(2,1)} %all_to_all.30), calls=%async_computation | async-start | bytes 8192 | tf_op jit(solution)/shard_map/all_to_all | solution.py:107
  641.5 1.1 copy-start.1
  641.5 1.2 copy-start.2
  1018.7 91.6 %all-to-all-start.1 = ((bf16[8,1,64]{2,1,0:T(2,128)(2,1)}), bf16[8,1,64]{2,1,0:T(2,128)(2,1)S(1)}, u32[]{:S(2)}, u32[]{:S(2)}) async-start(bf16[8,1,64]{2,1,0:T(2,128)(2,1)} %copy.166), calls=%async_computation.1 | async-start | bytes 8192 | tf_op jit(solution)/shard_map/all_to_all | solution.py:103
  1031.0 994.8 %all-reduce.7.cloned.1.call-start = ((), (), s32[]{:S(2)}) async-start(), calls=%async_computation.2 | async-start | bytes 2228224 | tf_op jit(solution)/shard_map/psum | solution.py:19
Sparse Core Ops, SparseCore 0:
  1726.9 298.9 all-reduce.6
where the time goes:
time: 2050 us; the launch traced here: 2040 us
  blocking collectives  1440 us (70%)
  local copies, waits for them, and re-layouts  352 us (17%)
  waiting for transfers between devices  169 us (8%)
  matrix products  32.6 us (2%)
  starting transfers between devices  24.1 us (1%)
    all_gather x1, blocking collectives, on_device(): lax.all_gather(cotangent, ('dp', 'space'), axis=0, tiled=True)  620 us
    all_gather x1, blocking collectives, on_device(): lax.all_gather(features, ('dp', 'space'), axis=0, tiled=True)  614 us
    while x424, local copies, waits for them, and re-layouts  291 us
    psum x1, waiting for transfers between devices, spread_2(): return lax.psum(kept, axis)  169 us
    psum x1, blocking collectives, spread_2(): return lax.psum(kept, axis)  129 us
    psum x1, blocking collectives, on_device(): lax.psum((moment_in, moment_out, conv_sum), ('dp', 'space'))  73.1 us
    reshape x16, local copies, waits for them, and re-layouts, patch_matrix(): jnp.stack(pieces, axis=1).reshape(channels * 27, planes * height * length)  43.1 us
  transfers between devices with their start and end apart: 5, of which 1 were waited for; matrix products, arithmetic and copies ran while one was open for 0% of the time, Pallas kernels for 0%

commit v1 on v0

--- a/solution.py
+++ b/solution.py
@@ -135,7 +135,12 @@
     conv_out = conv_out / cell_count
     conv_grad = conv_grad / cell_count
     all_features, all_cotangent = (
-        lax.all_gather(features, ("dp", "space"), axis=0, tiled=True),
+        jnp.concatenate(
+            lax.all_to_all(
+                jnp.stack([features] * lax.axis_size(("dp", "space"))), ("dp", "space"), 0, 0
+            ),
+            axis=0,
+        ),
         lax.all_gather(cotangent, ("dp", "space"), axis=0, tiled=True),
     )
     dense_in, dense_out, dense_grad = dense_moments_of(all_features, all_cotangent)

time: 2050 us -> 1450 us (0.71)
  blocking collectives: 1440 us -> 827 us
    all_gather x1 -> x0, blocking collectives: 614 us -> none  [on_device(): lax.all_gather(features, ('dp', 'space'), axis=0, tiled=True)]
  transfers between devices with their start and end apart: 5 -> 6, of which waited for: 1 -> 2; matrix products, arithmetic and copies ran while one was open for 0% -> 27% of each run, Pallas kernels for 0% -> 0%
where the time goes in v1:
time: 1450 us; the launch traced here: 1440 us
  blocking collectives  827 us (57%)
  local copies, waits for them, and re-layouts  356 us (25%)
  waiting for transfers between devices  166 us (11%)
  matrix products  32.6 us (2%)
  starting transfers between devices  32.4 us (2%)
  between operations  15.6 us (1%)
    all_gather x1, blocking collectives, on_device(): lax.all_gather(cotangent, ('dp', 'space'), axis=0, tiled=True)  620 us
    while x424, local copies, waits for them, and re-layouts  291 us
    psum x1, waiting for transfers between devices, spread_2(): return lax.psum(kept, axis)  161 us
    psum x1, blocking collectives, spread_2(): return lax.psum(kept, axis)  129 us
    psum x1, blocking collectives, on_device(): lax.psum((moment_in, moment_out, conv_sum), ('dp', 'space'))  78.5 us
    reshape x16, local copies, waits for them, and re-layouts, patch_matrix(): jnp.stack(pieces, axis=1).reshape(channels * 27, planes * height * length)  43.1 us
  transfers between devices with their start and end apart: 6, of which 2 were waited for; matrix products, arithmetic and copies ran while one was open for 27% of the time, Pallas kernels for 0%

profile of v1, /device:TPU:2, one launch (start us, length us, event | category | flops | bytes accessed | tf_op | source)
XLA Modules:
  0.0 1441.5 jit_solution(10379504702048349247)
XLA Ops:
  8.2 3.5 collective-permute-start
  11.7 4.5 collective-permute-start.1
  17.7 3.8 all-to-all-start
  21.5 619.8 %all-gather = bf16[256,1,128]{2,1,0:T(2,128)(2,1)S(1)} all-gather(bf16[1,1,128]{2,1,0:T(2,128)(2,1)} %bitcast.621), channel_id=1, replica_groups=mesh['dp'=32,'space'=8] {'dp','space'}, dimensions={0}, use_global_device_ids=true | all-gather | bytes 65792 | tf_op jit(solution)/shard_map/all_gather | solution.py:144
  642.7 185.2 %while.31 = (s32[]{:T(128)}, f32[108,108]{1,0:T(8,128)S(1)}, bf16[8,64]{1,0:T(8,128)(2,1)S(1)}, bf16[8,4,6,16,128]{4,3,2,1,0:T(8,128)(2,1)S(1)}, bf16[32,108]{1,...) while((s32[]{:T(128)}, f32[108,108]{1,0:T(8,128)S(1)}, bf16[8,64]{1,0:T(8,128)(2,1)S(1)}, ...), condition=%wide.region_12.13_spmd.clone, body=%wide.region_10.12_spmd.clone.sunk | while | flops 248798048 | bytes 15895667 | solution.py:100
  661.6 2.7 reshape.113
  684.7 2.7 reshape.113
  707.9 2.7 reshape.113
  731.0 2.7 reshape.113
  754.2 2.7 reshape.113
  777.3 2.7 reshape.113
  800.5 2.7 reshape.113
  823.6 2.7 reshape.113
  828.5 12.3 all-to-all-start.1
  840.9 4.7 all-to-all-done.1
  849.5 8.1 all-to-all-start.2
  857.8 190.2 %while.30 = (s32[]{:T(128)}, f32[32,32]{1,0:T(8,128)S(1)}, f32[32,108]{1,0:T(8,128)S(1)}, bf16[8,4,6,16,128]{4,3,2,1,0:T(8,128)(2,1)S(1)}, bf16[32,108]{1,0:T(8,...) while((s32[]{:T(128)}, f32[32,32]{1,0:T(8,128)S(1)}, ...), condition=%wide.region_1.2_spmd.clone, body=%wide.region_0.1_spmd.clone.sunk | while | flops 131081024 | bytes 15313904 | solution.py:130
  876.7 2.7 reshape.111
  900.4 2.7 reshape.111
  948.0 2.7 reshape.111
  1048.0 78.5 %all-reduce.2 = (f32[32,32]{1,0:T(8,128)S(1)}, f32[32,108]{1,0:T(8,128)S(1)}, f32[108,108]{1,0:T(8,128)S(1)}) all-reduce(f32[32,32]{1,0:T(8,128)S(1)} %get-tuple-element.174, f32[32,108]{1,0:T(8,128)S(1)} %get-tuple-element.175, f32[108,108]{1,0:T(8,128)S(1)} %get-tuple-element.176), channel_id=1, replica_groups=mesh['dp'=32,'space'=8] {'dp','space'}, use_global_device_ids=true, to_apply=%region_2.3 | all-reduce | flops 16144 | bytes 129152 | tf_op jit(solution)/shard_map/psum | solution.py:131
  1126.5 6.0 conditional.5
  1136.6 128.7 %all-reduce.3 = (f32[32,32]{1,0:T(8,128)S(1)}, f32[108,108]{1,0:T(8,128)S(1)}) all-reduce(f32[32,32]{1,0:T(8,128)S(1)} %broadcast_select_fusion.3, f32[108,108]{1,0:T(8,128)S(1)} %broadcast_select_fusion.2), channel_id=1, replica_groups=mesh['dp'=32,'space'=8] {'dp'}, use_global_device_ids=true, to_apply=%region_8.9 | all-reduce | flops 12688 | bytes 101504 | tf_op jit(solution)/shard_map/psum | solution.py:19
  1266.5 161.2 %all-reduce.7.cloned.1.call-done = (f32[512,512]{1,0:T(8,128)}, f32[128,128]{1,0:T(8,128)}) async-done(((f32[512,512]{1,0:T(8,128)}, f32[128,128]{1,0:T(8,128)}), (f32[512,512]{1,0:T(8,128)}, f32[128,128]{1,0:T(8,128)})) %all-reduce.7.cloned.1.call-update) | async-done | bytes 1114128 | tf_op jit(solution)/shard_map/psum | solution.py:19
  (629 shorter events, 368.4 us)
Async XLA Ops:
  7.2 9.0 copy-start
  8.2 634.0 %collective-permute-start = (bf16[8,4,1,16,128]{4,3,2,1,0:T(8,128)(2,1)S(1)}, bf16[8,4,1,16,128]{4,3,2,1,0:T(8,128)(2,1)S(1)}, u32[]{:S(2)}, u32[]{:S(2)}) collective-permute-start(bf16[8,4,1,16,128]{4,3,2,1,0:T(8,128)(2,1)S(1)} %get-tuple-element.247), channel_id=1, source_target_pairs={{0,1},{1,2},{2,3},{3,4},{4,5},{5,6},{6,7},{8,9},{9,10},{10,11},{11... | collective-permute-start | bytes 393224 | tf_op jit(solution)/shard_map/ppermute | solution.py:29
  11.7 631.0 %collective-permute-start.1 = (bf16[8,4,1,16,128]{4,3,2,1,0:T(8,128)(2,1)S(1)}, bf16[8,4,1,16,128]{4,3,2,1,0:T(8,128)(2,1)S(1)}, u32[]{:S(2)}, u32[]{:S(2)}) collective-permute-start(bf16[8,4,1,16,128]{4,3,2,1,0:T(8,128)(2,1)S(1)} %get-tuple-element.246), channel_id=1, source_target_pairs={{1,0},{2,1},{3,2},{4,3},{5,4},{6,5},{7,6},{9,8},{10,9},{11,10},{12... | collective-permute-start | bytes 393224 | tf_op jit(solution)/shard_map/ppermute | solution.py:30
  17.7 810.8 %all-to-all-start = ((bf16[1,8,64]{2,0,1:T(2,128)(2,1)}), bf16[1,8,64]{2,0,1:T(2,128)(2,1)S(1)}, u32[]{:S(2)}, u32[]{:S(2)}) async-start(bf16[1,8,64]{2,0,1:T(2,128)(2,1)} %all_to_all.31), calls=%async_computation | async-start | bytes 8192 | tf_op jit(solution)/shard_map/all_to_all | solution.py:107
  641.5 1.1 copy-start.1
  641.5 1.2 copy-start.2
  828.5 17.1 %all-to-all-start.1 = ((bf16[8,1,64]{2,1,0:T(2,128)(2,1)}), bf16[8,1,64]{2,1,0:T(2,128)(2,1)S(1)}, u32[]{:S(2)}, u32[]{:S(2)}) async-start(bf16[8,1,64]{2,1,0:T(2,128)(2,1)} %copy.166), calls=%async_computation.1 | async-start | bytes 8192 | tf_op jit(solution)/shard_map/all_to_all | solution.py:103
  849.5 283.0 %all-to-all-start.2 = ((bf16[256,2,256]{2,1,0:T(2,128)(2,1)}), bf16[256,2,256]{2,1,0:T(2,128)(2,1)}, u32[]{:S(2)}, u32[]{:S(2)}) async-start(bf16[256,2,256]{2,1,0:T(2,128)(2,1)} %reshape.106), calls=%async_computation.2 | async-start | bytes 524288 | tf_op jit(solution)/shard_map/all_to_all | solution.py:139
  857.6 570.2 %all-reduce.7.cloned.1.call-start = ((), (), s32[]{:S(2)}) async-start(), calls=%async_computation.3 | async-start | bytes 2228224 | tf_op jit(solution)/shard_map/psum | solution.py:19
Sparse Core Ops, SparseCore 0:
  1136.7 291.0 all-reduce.6
